TPU v7x, 512 devices: a whole 4x8x8 slice. The times are simulated.
512 devices in a mesh: line: 16 (over y, core), cross: 32 (over z, x).
Axes of the slice: x: 4, y: 8, z: 8, core: 2. Of those that a mesh axis runs over, the one named last changes fastest.
Arguments:
- jacobian: float32 [5, 5, 512, 4096], P(None, None, 'line', 'cross'), may hold values from -41 to 121, as said below
- time_step: float32 [512, 4096], P('line', 'cross'), may hold values from 2 to 8
- source: bfloat16 [5, 512, 4096], P(None, 'line', 'cross'), may hold values from -12 to 15
- cross_flux: bfloat16 [5, 512, 4096], P(None, 'line', 'cross'), may hold values from -12 to 12
Outputs:
- update: float32 [5, 512, 4096], P(None, 'line', 'cross')
Inputs may be any that keep to these rules, and one draw needn't show every extreme that they name: Every 5 x 5 block of jacobian is symmetric, and for every line the system matrix of the last step has a positive definite symmetric part.
All inputs are finite; a program needn't handle non-finite values.
Results may differ from a plain program's by a relative error of at most 0.0003.
Values may be sent and summed in bfloat16 or wider, within the bound.
No kernel may reach another device: no remote copies, remote signals or barrier semaphores. Data moves between devices by JAX's collectives and lax.ppermute only.
A program may use at most 64 MiB of HBM per device.

v0:
```python
import jax
import jax.numpy as jnp
from jax import lax
from jax.experimental import pallas as pl
from jax.experimental.pallas import tpu as pltpu
from jax.sharding import PartitionSpec as P

NZ = 8
damping = 0.05

CHUNKS = 8
CELLS = 4
LANES = 128
SENT = 125
ROWS = 128
INV, LOW, UPP, VLOW, VUPP = (25 * k for k in range(5))
STAGE = 125
N = range(5)


def tile(ref, number):
    return ref[8 * number : 8 * number + 8, :]


def block(ref, base):
    return [[tile(ref, base + 5 * a + b) for b in N] for a in N]


def vector(ref, base):
    return [tile(ref, base + a) for a in N]


def keep(ref, base, matrix):
    for a in N:
        for b in N:
            ref[8 * (base + 5 * a + b) : 8 * (base + 5 * a + b) + 8, :] = matrix[a][b]


def keep_vector(ref, base, values):
    for a in N:
        ref[8 * (base + a) : 8 * (base + a) + 8, :] = values[a]


def total(terms):
    result = terms[0]
    for term in terms[1:]:
        result = result + term
    return result


def mm(left, right):
    return [[total([left[a][k] * right[k][b] for k in N]) for b in N] for a in N]


def mv(left, right):
    return [total([left[a][k] * right[k] for k in N]) for a in N]


def plus(left, right):
    return [[left[a][b] + right[a][b] for b in N] for a in N]


def minus(left, right):
    return [[left[a][b] - right[a][b] for b in N] for a in N]


def negative(matrix):
    return [[-matrix[a][b] for b in N] for a in N]


def vplus(left, right):
    return [left[a] + right[a] for a in N]


def vminus(left, right):
    return [left[a] - right[a] for a in N]


def scaled(factor, matrix):
    return [[factor * matrix[a][b] for b in N] for a in N]


def shifted(matrix, amount):
    return [[matrix[a][b] + amount if a == b else matrix[a][b] for b in N] for a in N]


def turn(value, count):
    return pltpu.roll(value, count % CHUNKS, axis=0)


def flipped(matrix):
    return [[matrix[b][a] for b in N] for a in N]


def mturn(matrix, count):
    return [[turn(matrix[a][b], count) for b in N] for a in N]


def vturn(values, count):
    return [turn(values[a], count) for a in N]


def inverse(matrix):
    m = [list(row) for row in matrix]
    for k in N:
        pivot = 1.0 / m[k][k]
        for b in N:
            m[k][b] = pivot if b == k else m[k][b] * pivot
        for a in N:
            if a != k:
                factor = m[a][k]
                for b in N:
                    m[a][b] = -factor * pivot if b == k else m[a][b] - factor * m[k][b]
    return m


def inverse_and_solved(matrix, *sides):
    m = [list(row) + [side[a][b] for side in sides for b in N] for a, row in enumerate(matrix)]
    width = len(m[0])
    for k in N:
        pivot = 1.0 / m[k][k]
        for b in range(width):
            m[k][b] = pivot if b == k else m[k][b] * pivot
        for a in N:
            if a != k:
                factor = m[a][k]
                for b in range(width):
                    m[a][b] = -factor * pivot if b == k else m[a][b] - factor * m[k][b]
    return [[row[at : at + 5] for row in m] for at in range(0, width, 5)]


def half_jacobian(jac_ref, cell):
    half = [[None] * 5 for _ in N]
    for a in N:
        for b in range(a, 5):
            half[a][b] = half[b][a] = 0.5 * jac_ref[a, b, pl.ds(cell, CHUNKS, stride=CELLS), :]
    return half


def half_before(half_last):
    first = lax.broadcasted_iota(jnp.int32, (CHUNKS, LANES), 0) == 0
    result = [[None] * 5 for _ in N]
    for a in N:
        for b in range(a, 5):
            outside = 1.0 - damping if a == b else 0.0
            result[a][b] = result[b][a] = jnp.where(first, outside, turn(half_last[a][b], 1))
    return result


def diagonal(step_ref, cell):
    return 1.0 / step_ref[pl.ds(cell, CHUNKS, stride=CELLS), :] + 2.0 * damping


def stage(fac_ref, base, low, own, nxt, upp, distance):
    inv = inverse(plus(own, nxt))
    vlow = mm(inv, low)
    vupp = mm(inv, upp)
    keep(fac_ref, base + INV, inv)
    keep(fac_ref, base + LOW, low)
    keep(fac_ref, base + UPP, upp)
    keep(fac_ref, base + VLOW, vlow)
    keep(fac_ref, base + VUPP, vupp)
    own = minus(own, mm(low, mturn(vupp, distance)))
    nxt = minus(nxt, mm(upp, mturn(vlow, -distance)))
    low = negative(mm(low, mturn(vlow, distance)))
    upp = negative(mm(upp, mturn(vupp, -distance)))
    return low, own, nxt, upp


def stage_rhs(fac_ref, base, own, nxt, distance):
    value = mv(block(fac_ref, base + INV), vplus(own, nxt))
    own = vminus(own, mv(block(fac_ref, base + LOW), vturn(value, distance)))
    nxt = vminus(nxt, mv(block(fac_ref, base + UPP), vturn(value, -distance)))
    return value, own, nxt


def stage_back(fac_ref, base, value, before, after):
    return vminus(
        vminus(value, mv(block(fac_ref, base + VLOW), before)), mv(block(fac_ref, base + VUPP), after)
    )


def rows_of_last(ref, group):
    return ref[pl.ds(64 * group + 7, 8, stride=8), :]


def merge(fac_ref, base, former, latter, upp, low):
    head_head, head_tail, tail_head, tail_tail = former
    inv_head, carry, reach = inverse_and_solved(latter[0], low, latter[1])
    inv_tail, tail_by_head, tail_by_tail = inverse_and_solved(
        plus(tail_tail, mm(upp, carry)), tail_head, mm(upp, reach)
    )
    head_by_head = mm(carry, tail_by_head)
    head_by_tail = minus(reach, mm(carry, tail_by_tail))
    for number, kept in enumerate(
        (
            inv_head,
            carry,
            inv_tail,
            upp,
            head_tail,
            latter[2],
            tail_by_head,
            tail_by_tail,
            head_by_head,
            head_by_tail,
        )
    ):
        keep(fac_ref, base + 25 * number, kept)
    return (
        minus(head_head, mm(head_tail, tail_by_head)),
        mm(head_tail, tail_by_tail),
        negative(mm(latter[2], head_by_head)),
        minus(latter[3], mm(latter[2], head_by_tail)),
    )


def merge_rhs(fac_ref, base, former, latter):
    head = mv(block(fac_ref, base), latter[0])
    tail = mv(block(fac_ref, base + 50), vminus(former[1], mv(block(fac_ref, base + 75), head)))
    head = vplus(head, mv(block(fac_ref, base + 25), tail))
    return (
        tail,
        head,
        vminus(former[0], mv(block(fac_ref, base + 100), tail)),
        vminus(latter[1], mv(block(fac_ref, base + 125), head)),
    )


def merge_back(fac_ref, base, tail, head, first, last):
    tail = vplus(
        vminus(tail, mv(block(fac_ref, base + 150), first)), mv(block(fac_ref, base + 175), last)
    )
    head = vminus(
        vminus(head, mv(block(fac_ref, base + 200), first)), mv(block(fac_ref, base + 225), last)
    )
    return tail, head


def rows_of_first(ref, group):
    return ref[pl.ds(64 * group, 8, stride=8), :]


MERGES = ((1, 200), (2, 450), (4, 700))
CLOSE = 950
TILES = 1050


def factor_kernel(jac_ref, step_ref, fac_ref, pack_ref, end_ref):
    e = damping
    h0 = half_jacobian(jac_ref, 0)
    h1 = half_jacobian(jac_ref, 1)
    h2 = half_jacobian(jac_ref, 2)
    h3 = half_jacobian(jac_ref, 3)
    d1 = diagonal(step_ref, 1)
    d2 = diagonal(step_ref, 2)
    h0p, h1p, h2p, h3p = shifted(h0, e), shifted(h1, e), shifted(h2, e), shifted(h3, e)
    h0m, h1m, h2m, h3m = shifted(h0, -e), shifted(h1, -e), shifted(h2, -e), shifted(h3, -e)
    inv = inverse(shifted(mm(h2m, h1p), d1 * d2))
    by_low = mm(inv, h0p)
    by_upp = mm(inv, mm(h2m, h3m))
    by_end = mm(flipped(inv), h3m)
    pair = mm(h2p, h1p)
    group = (
        shifted(mm(h1m, scaled(d2, by_low)), diagonal(step_ref, 0)),
        mm(h1m, by_upp),
        negative(mm(pair, by_low)),
        shifted(mm(scaled(d1, h2p), by_end), diagonal(step_ref, 3)),
    )
    keep(fac_ref, 0, inv)
    keep(fac_ref, 25, by_low)
    keep(fac_ref, 50, by_upp)
    keep(fac_ref, 75, by_end)
    for distance, base in MERGES:
        latter = tuple(mturn(part, -distance) for part in group)
        group = merge(fac_ref, base, group, latter, mturn(h0m, -distance), mturn(h3p, 1 - distance))
    head_head, head_tail, tail_head, tail_tail = group
    inv = inverse(head_head)
    reach = mm(inv, head_tail)
    through = mm(tail_head, inv)
    into = mm(h0m, inv)
    keep(fac_ref, CLOSE, inv)
    keep(fac_ref, CLOSE + 25, reach)
    keep(fac_ref, CLOSE + 50, through)
    keep(fac_ref, CLOSE + 75, into)
    keep(end_ref, 0, through)
    keep(end_ref, 25, minus(tail_tail, mm(tail_head, reach)))
    keep(end_ref, 50, into)
    keep(end_ref, 75, negative(mm(h0m, reach)))
    place = 100
    for a in N:
        for b in range(a, 5):
            end_ref[8 * place : 8 * place + 8, :] = turn(h3p[a][b], 1)
            place += 1
    for number in range(15):
        pack_ref[8 * number : 8 * number + 8, :] = rows_of_first(end_ref, number)


def rhs_kernel(
    jac_ref, step_ref, src_ref, flux_ref, before_ref, after_ref, fac_ref, part_ref, pack_ref, val_ref, res_ref, end_ref
):
    e = damping
    lane = lax.broadcasted_iota(jnp.int32, (CHUNKS * CELLS, LANES), 1)
    for a in N:
        flux = flux_ref[a].astype(jnp.float32)
        upper = pltpu.roll(jnp.where(lane < NZ, after_ref[a].astype(jnp.float32), flux), LANES - NZ, axis=1)
        lower = pltpu.roll(jnp.where(lane >= LANES - NZ, before_ref[a].astype(jnp.float32), flux), NZ, axis=1)
        res_ref[a] = src_ref[a].astype(jnp.float32) - 0.5 * (upper - lower)
    r0, r1, r2, r3 = ([res_ref[a, pl.ds(cell, CHUNKS, stride=CELLS), :] for a in N] for cell in range(CELLS))
    h1 = half_jacobian(jac_ref, 1)
    h2 = half_jacobian(jac_ref, 2)
    d1 = diagonal(step_ref, 1)
    d2 = diagonal(step_ref, 2)
    inv = block(fac_ref, 0)
    part = mv(inv, r1)
    x1 = vminus([d2 * value for value in part], mv(inv, mv(shifted(h2, -e), r2)))
    x2 = vplus(mv(shifted(h1, e), part), [d1 * value for value in mv(flipped(inv), r2)])
    keep_vector(val_ref, 0, x1)
    keep_vector(val_ref, 5, x2)
    head = vminus(r0, mv(shifted(h1, -e), x1))
    tail = vplus(r3, mv(shifted(h2, e), x2))
    place = 10
    for distance, base in MERGES:
        latter = (vturn(head, -distance), vturn(tail, -distance))
        inner_tail, inner_head, head, tail = merge_rhs(fac_ref, base, (head, tail), latter)
        keep_vector(val_ref, place, inner_tail)
        keep_vector(val_ref, place + 5, inner_head)
        place += 10
    keep_vector(val_ref, place, mv(block(fac_ref, CLOSE), head))
    end_ref[...] = jnp.zeros_like(end_ref)
    keep_vector(end_ref, 3, vminus(tail, mv(block(fac_ref, CLOSE + 50), head)))
    keep_vector(end_ref, 8, [-value for value in mv(block(fac_ref, CLOSE + 75), head)])
    pack_ref[:112, :] = part_ref[:112, :]
    row = lax.broadcasted_iota(jnp.int32, (8, LANES), 0)
    pack_ref[112:120, :] = jnp.where(row < 3, part_ref[112:120, :], rows_of_first(end_ref, 0))
    pack_ref[120:125, :] = rows_of_first(end_ref, 1)[:5]


def solve_kernel(sent_ref, jac_ref, step_ref, fac_ref, val_ref, out_ref, all_ref, red_ref, x_ref, w_ref):
    e = damping
    for device in range(16):
        all_ref[ROWS * device : ROWS * device + SENT, :] = sent_ref[device]
    row = lax.broadcasted_iota(jnp.int32, (CHUNKS, LANES), 0)

    def packed(parity, number):
        return all_ref[pl.ds(parity * ROWS + number, 8, stride=2 * ROWS), :]

    def packed_block(parity, base):
        return [[packed(parity, base + 5 * a + b) for b in N] for a in N]

    def packed_vector(parity, base):
        return [packed(parity, base + a) for a in N]

    def packed_symmetric(parity, base):
        result = [[None] * 5 for _ in N]
        for a in N:
            for b in range(a, 5):
                result[a][b] = result[b][a] = packed(parity, base)
                base += 1
        return result

    m_even = packed_symmetric(0, 100)
    m_odd = packed_symmetric(1, 100)
    inv = inverse(plus(packed_block(0, 25), mm(packed_block(1, 50), m_even)))
    vlow = mm(inv, packed_block(0, 0))
    vupp = mm(inv, packed_block(1, 75))
    value = mv(inv, vplus(packed_vector(0, 115), packed_vector(1, 120)))
    keep(red_ref, VLOW, vlow)
    keep(red_ref, VUPP, vupp)
    keep_vector(x_ref, 4, value)
    cross = mm(packed_block(1, 0), m_even)
    own = minus(packed_block(1, 25), mm(cross, vupp))
    low = negative(mm(cross, vlow))
    own_rhs = vminus(packed_vector(1, 115), mv(cross, value))
    back = packed_block(0, 75)
    nxt = minus(packed_block(0, 50), mm(back, vlow))
    upp = negative(mm(back, vupp))
    nxt_rhs = vminus(packed_vector(0, 120), mv(back, value))
    first, last = row == 0, row == CHUNKS - 1
    low = mm(low, mturn(m_odd, 1))
    low = [[jnp.where(first, 0.0, low[a][b]) for b in N] for a in N]
    nxt = mm(mturn(nxt, -1), m_odd)
    nxt = [[jnp.where(last, 0.0, nxt[a][b]) for b in N] for a in N]
    upp = [[jnp.where(last, 0.0, turn(upp[a][b], -1)) for b in N] for a in N]
    nxt_rhs = [jnp.where(last, 0.0, turn(nxt_rhs[a], -1)) for a in N]
    levels = ((1, 1), (2, 2), (3, 4))
    values = []
    for number, distance in levels:
        low, own, nxt, upp = stage(red_ref, number * STAGE, low, own, nxt, upp, distance)
        value, own_rhs, nxt_rhs = stage_rhs(red_ref, number * STAGE, own_rhs, nxt_rhs, distance)
        values.append(value)
    x = mv(inverse(plus(own, nxt)), vplus(own_rhs, nxt_rhs))
    for number, distance in reversed(levels):
        found = stage_back(red_ref, number * STAGE, values[number - 1], vturn(x, distance), vturn(x, -distance))
        chosen = (row % (2 * distance)) == distance - 1
        x = [jnp.where(chosen, found[a], x[a]) for a in N]
    w_odd = mv(m_odd, x)
    before = [jnp.where(first, 0.0, turn(w_odd[a], 1)) for a in N]
    x_even = stage_back(red_ref, 0, vector(x_ref, 4), before, x)
    w_even = mv(m_even, x_even)
    position = lax.axis_index("line")
    half, odd = position // 2, position % 2
    is_odd = odd == 1
    for a in N:
        w_ref[8 * a : 8 * a + 8, :] = jnp.where(is_odd, w_even[a], before[a])
        x_ref[8 * a : 8 * a + 8, :] = jnp.where(is_odd, x[a], x_even[a])
    ends = [jnp.broadcast_to(x_ref[pl.ds(8 * a + half, 1), :], (CHUNKS, LANES)) for a in N]
    w = [jnp.broadcast_to(w_ref[pl.ds(8 * a + half, 1), :], (CHUNKS, LANES)) for a in N]

    last = ends
    first = vplus(vector(val_ref, 40), vminus(mv(block(fac_ref, CLOSE), w), mv(block(fac_ref, CLOSE + 25), last)))
    place = 30
    for distance, base in reversed(MERGES):
        tail, head = merge_back(fac_ref, base, vector(val_ref, place), vector(val_ref, place + 5), first, last)
        place -= 10
        latter = (row % (2 * distance)) >= distance
        first = [jnp.where(latter, turn(head[a], distance), first[a]) for a in N]
        last = [jnp.where(latter, turn(last[a], distance), tail[a]) for a in N]
    d1 = diagonal(step_ref, 1)
    d2 = diagonal(step_ref, 2)
    part = mv(block(fac_ref, 25), first)
    x1 = vplus(vplus(vector(val_ref, 0), [d2 * value for value in part]), mv(block(fac_ref, 50), last))
    far = mv(block(fac_ref, 75), last)
    near = mv(shifted(half_jacobian(jac_ref, 1), e), part)
    x2 = vplus(vector(val_ref, 5), vminus(near, [d1 * value for value in far]))
    for a in N:
        out_ref[a, pl.ds(0, CHUNKS, stride=CELLS), :] = first[a]
        out_ref[a, pl.ds(1, CHUNKS, stride=CELLS), :] = x1[a]
        out_ref[a, pl.ds(2, CHUNKS, stride=CELLS), :] = x2[a]
        out_ref[a, pl.ds(3, CHUNKS, stride=CELLS), :] = last[a]


INTERPRET = False


def run(kernel, name, outs, args, scratch):
    inside = pl.BlockSpec(memory_space=pltpu.VMEM)
    if INTERPRET:
        shapes = [jax.ShapeDtypeStruct(shape, jnp.float32) for shape in outs]
    else:
        args = [pltpu.with_memory_space_constraint(arg, pltpu.VMEM) for arg in args]
        shapes = [pltpu.VMEM(shape, jnp.float32) for shape in outs]
    return pl.pallas_call(
        kernel,
        out_shape=shapes,
        in_specs=[inside] * len(args),
        out_specs=[inside] * len(outs),
        scratch_shapes=[pltpu.VMEM(shape, jnp.float32) for shape in scratch],
        interpret=INTERPRET,
        compiler_params=pltpu.CompilerParams(vmem_limit_bytes=12 << 20),
        name=name,
    )(*args)


def shards(jacobian, time_step, source, cross_flux):
    count = lax.axis_size("cross")
    before = lax.ppermute(cross_flux, "cross", [(i, i + 1) for i in range(count - 1)])
    after = lax.ppermute(cross_flux, "cross", [(i + 1, i) for i in range(count - 1)])
    factors, part = run(
        factor_kernel, "factor", [(TILES * 8, LANES), (120, LANES)], [jacobian, time_step], [(120 * 8, LANES)]
    )
    packet, values = run(
        rhs_kernel,
        "right_side",
        [(SENT, LANES), (45 * 8, LANES)],
        [jacobian, time_step, source, cross_flux, before, after, factors, part],
        [(5, CHUNKS * CELLS, LANES), (16 * 8, LANES)],
    )
    packets = lax.all_gather(packet, "line", axis=0)
    return run(
        solve_kernel,
        "solve",
        [(5, CHUNKS * CELLS, LANES)],
        [packets, jacobian, time_step, factors, values],
        [(16 * ROWS, LANES), (4 * STAGE * 8, LANES), (16 * 8, LANES), (5 * 8, LANES)],
    )[0]


def solution(mesh):
    placed = (
        P(None, None, "line", "cross"),
        P("line", "cross"),
        P(None, "line", "cross"),
        P(None, "line", "cross"),
    )
    return jax.shard_map(
        shards, mesh=mesh, in_specs=placed, out_specs=P(None, "line", "cross"), check_vma=False
    )
```

profile of v0, /device:TPU:199, one launch (start us, length us, event | category | flops | bytes accessed | tf_op | source)
XLA Modules:
  0.0 41.0 jit_solution(84617473419653421)
XLA Ops:
  0.0 5.1 %collective-permute-start = (bf16[5,32,128]{2,1,0:T(8,128)(2,1)}, bf16[5,32,128]{2,1,0:T(8,128)(2,1)S(1)}, u32[]{:S(2)}, u32[]{:S(2)}) collective-permute-start(bf16[5,32,128]{2,1,0:T(8,128)(2,1)} %flux_ref.1), channel_id=1, source_target_pairs={{0,1},{1,2},{2,3},{3,4},{4,5},{5,6},{6,7},{7,8},{8,9},{9,10},{10,1... | collective-permute-start | bytes 122888 | tf_op jit(solution)/shard_map/ppermute | solution.py:457
  5.1 1.9 %collective-permute-start.1 = (bf16[5,32,128]{2,1,0:T(8,128)(2,1)}, bf16[5,32,128]{2,1,0:T(8,128)(2,1)S(1)}, u32[]{:S(2)}, u32[]{:S(2)}) collective-permute-start(bf16[5,32,128]{2,1,0:T(8,128)(2,1)} %flux_ref.1), channel_id=1, source_target_pairs={{1,0},{2,1},{3,2},{4,3},{5,4},{6,5},{7,6},{8,7},{9,8},{10,9},{11,1... | collective-permute-start | bytes 122888 | tf_op jit(solution)/shard_map/ppermute | solution.py:458
  7.1 0.0 copy-start
  7.1 1.0 %copy-done = f32[5,5,32,128]{3,2,1,0:T(8,128)S(1)} copy-done((f32[5,5,32,128]{3,2,1,0:T(8,128)S(1)}, f32[5,5,32,128]{3,2,1,0:T(8,128)}, u32[]{:S(2)}) %copy-start) | copy-done | bytes 409624
  8.1 0.0 copy-start.1
  8.1 0.7 %copy-done.1 = f32[32,128]{1,0:T(8,128)S(1)} copy-done((f32[32,128]{1,0:T(8,128)S(1)}, f32[32,128]{1,0:T(8,128)}, u32[]{:S(2)}) %copy-start.1) | copy-done | bytes 16408
  8.8 2.3 %factor.1 = (f32[8400,128]{1,0:T(8,128)S(1)}, f32[120,128]{1,0:T(8,128)S(1)}) custom-call(f32[5,5,32,128]{3,2,1,0:T(8,128)S(1)} %copy-done, f32[32,128]{1,0:T(8,128)S(1)} %copy-done.1), custom_call_target="tpu_custom_call" | custom-call | tf_op jit(solution)/shard_map/factor/pallas_call | solution.py:443
  11.0 0.0 collective-permute-done.before_ref
  11.1 2.4 %collective-permute-done.1.after_ref = bf16[5,32,128]{2,1,0:T(8,128)(2,1)S(1)} collective-permute-done((bf16[5,32,128]{2,1,0:T(8,128)(2,1)}, bf16[5,32,128]{2,1,0:T(8,128)(2,1)S(1)}, u32[]{:S(2)}, u32[]{:S(2)}) %collective-permute-start.1) | collective-permute-done | bytes 40992 | tf_op jit(solution)/shard_map/ppermute | solution.py:458
  13.4 0.0 copy-start.2
  13.4 0.7 %copy-done.2 = f32[32,128]{1,0:T(8,128)S(1)} copy-done((f32[32,128]{1,0:T(8,128)S(1)}, f32[32,128]{1,0:T(8,128)}, u32[]{:S(2)}) %copy-start.2) | copy-done | bytes 16408
  14.1 0.0 copy-start.3
  14.1 0.8 %copy-done.3 = bf16[5,32,128]{2,1,0:T(8,128)(2,1)S(1)} copy-done((bf16[5,32,128]{2,1,0:T(8,128)(2,1)S(1)}, bf16[5,32,128]{2,1,0:T(8,128)(2,1)}, u32[]{:S(2)}) %copy-start.3) | copy-done | bytes 40984
  14.9 0.0 copy-start.4
  14.9 0.8 %copy-done.4 = bf16[5,32,128]{2,1,0:T(8,128)(2,1)S(1)} copy-done((bf16[5,32,128]{2,1,0:T(8,128)(2,1)S(1)}, bf16[5,32,128]{2,1,0:T(8,128)(2,1)}, u32[]{:S(2)}) %copy-start.4) | copy-done | bytes 40984
  15.7 0.3 right_side.1
  16.0 22.5 %all-gather.1.sent_ref = f32[16,125,128]{2,1,0:T(8,128)S(1)} all-gather(f32[1,125,128]{2,1,0:T(8,128)S(1)} %bitcast.1), channel_id=2, replica_groups=mesh['line'=16,'cross'=32] {'line'}, dimensions={0}, use_global_device_ids=true | all-gather | bytes 1088000 | tf_op jit(solution)/shard_map/all_gather | solution.py:469
  38.5 1.9 %solve.1 = f32[5,32,128]{2,1,0:T(8,128)S(1)} custom-call(f32[16,125,128]{2,1,0:T(8,128)S(1)} %all-gather.1.sent_ref, f32[5,5,32,128]{3,2,1,0:T(8,128)S(1)} %copy-done, f32[32,128]{1,0:T(8,128)S(1)} %copy-done.2, f32[8400,128]{1,0:T(8,128)S(1)} %get-tuple-element.9.fac_ref, f32[360,128]{1,0:T(8,128)S(1)} %get-tuple-element.12.val_ref), custom_call_target="tpu_custom_call" | custom-call | tf_op jit(solution)/shard_map/solve/pallas_call | solution.py:443
  40.4 0.6 %copy.5 = f32[5,32,128]{2,1,0:T(8,128)} copy(f32[5,32,128]{2,1,0:T(8,128)S(1)} %solve.1) | data formatting | bytes 163840
Async XLA Ops:
  0.0 11.0 %collective-permute-start = (bf16[5,32,128]{2,1,0:T(8,128)(2,1)}, bf16[5,32,128]{2,1,0:T(8,128)(2,1)S(1)}, u32[]{:S(2)}, u32[]{:S(2)}) collective-permute-start(bf16[5,32,128]{2,1,0:T(8,128)(2,1)} %flux_ref.1), channel_id=1, source_target_pairs={{0,1},{1,2},{2,3},{3,4},{4,5},{5,6},{6,7},{7,8},{8,9},{9,10},{10,1... | collective-permute-start | bytes 122888 | tf_op jit(solution)/shard_map/ppermute | solution.py:457
  5.1 8.3 %collective-permute-start.1 = (bf16[5,32,128]{2,1,0:T(8,128)(2,1)}, bf16[5,32,128]{2,1,0:T(8,128)(2,1)S(1)}, u32[]{:S(2)}, u32[]{:S(2)}) collective-permute-start(bf16[5,32,128]{2,1,0:T(8,128)(2,1)} %flux_ref.1), channel_id=1, source_target_pairs={{1,0},{2,1},{3,2},{4,3},{5,4},{6,5},{7,6},{8,7},{9,8},{10,9},{11,1... | collective-permute-start | bytes 122888 | tf_op jit(solution)/shard_map/ppermute | solution.py:458
  7.1 1.0 %copy-start = (f32[5,5,32,128]{3,2,1,0:T(8,128)S(1)}, f32[5,5,32,128]{3,2,1,0:T(8,128)}, u32[]{:S(2)}) copy-start(f32[5,5,32,128]{3,2,1,0:T(8,128)} %jac_ref.5) | copy-start | bytes 1228804
  8.1 0.7 %copy-start.1 = (f32[32,128]{1,0:T(8,128)S(1)}, f32[32,128]{1,0:T(8,128)}, u32[]{:S(2)}) copy-start(f32[32,128]{1,0:T(8,128)} %step_ref.5) | copy-start | bytes 49156
  13.4 0.7 %copy-start.2 = (f32[32,128]{1,0:T(8,128)S(1)}, f32[32,128]{1,0:T(8,128)}, u32[]{:S(2)}) copy-start(f32[32,128]{1,0:T(8,128)} %step_ref.5) | copy-start | bytes 49156
  14.1 0.8 %copy-start.3 = (bf16[5,32,128]{2,1,0:T(8,128)(2,1)S(1)}, bf16[5,32,128]{2,1,0:T(8,128)(2,1)}, u32[]{:S(2)}) copy-start(bf16[5,32,128]{2,1,0:T(8,128)(2,1)} %src_ref.1) | copy-start | bytes 122884
  14.9 0.8 %copy-start.4 = (bf16[5,32,128]{2,1,0:T(8,128)(2,1)S(1)}, bf16[5,32,128]{2,1,0:T(8,128)(2,1)}, u32[]{:S(2)}) copy-start(bf16[5,32,128]{2,1,0:T(8,128)(2,1)} %flux_ref.1) | copy-start | bytes 122884
where the time goes:
time: 41.4 us; the launch traced here: 41 us
  blocking collectives  22.5 us (54%)
  starting transfers between devices  7.04 us (17%)
  local copies, waits for them, and re-layouts  4.62 us (11%)
  Pallas kernels  4.48 us (11%)
  waiting for transfers between devices  2.35 us (6%)
    all_gather x1, blocking collectives, shards(): packets = lax.all_gather(packet, 'line', axis=0)  22.5 us
    ppermute x1, starting transfers between devices, shards(): lax.ppermute(cross_flux, 'cross', [(i, i + 1) for i in range(count - 1)])  5.12 us
    unnamed x11, local copies, waits for them, and re-layouts  4.62 us
    pallas_call x3, Pallas kernels, run(): pl.pallas_call(kernel, out_shape=shapes, in_specs=[inside] * len(args), o...  4.48 us
    ppermute x1, waiting for transfers between devices, shards(): lax.ppermute(cross_flux, 'cross', [(i + 1, i) for i in range(count - 1)])  2.35 us
    ppermute x1, starting transfers between devices, shards(): lax.ppermute(cross_flux, 'cross', [(i + 1, i) for i in range(count - 1)])  1.92 us
  transfers between devices with their start and end apart: 2, of which 1 were waited for; matrix products, arithmetic and copies ran while one was open for 0% of the time, Pallas kernels for 6%

commit v1 on v0

--- a/solution.py
+++ b/solution.py
@@ -152,9 +152,7 @@
 
 
 def stage(fac_ref, base, low, own, nxt, upp, distance):
-    inv = inverse(plus(own, nxt))
-    vlow = mm(inv, low)
-    vupp = mm(inv, upp)
+    inv, vlow, vupp = inverse_and_solved(plus(own, nxt), low, upp)
     keep(fac_ref, base + INV, inv)
     keep(fac_ref, base + LOW, low)
     keep(fac_ref, base + UPP, upp)
@@ -178,10 +176,6 @@
     return vminus(
         vminus(value, mv(block(fac_ref, base + VLOW), before)), mv(block(fac_ref, base + VUPP), after)
     )
-
-
-def rows_of_last(ref, group):
-    return ref[pl.ds(64 * group + 7, 8, stride=8), :]
 
 
 def merge(fac_ref, base, former, latter, upp, low):
@@ -237,16 +231,37 @@
     return tail, head
 
 
-def rows_of_first(ref, group):
-    return ref[pl.ds(64 * group, 8, stride=8), :]
-
-
-MERGES = ((1, 200), (2, 450), (4, 700))
-CLOSE = 950
-TILES = 1050
-
-
-def factor_kernel(jac_ref, step_ref, fac_ref, pack_ref, end_ref):
+def rows_of_last(ref, group):
+    return ref[pl.ds(64 * group + CHUNKS - WIDTH, 8, stride=8), :]
+
+
+WIDTH = 2
+MERGES = tuple((1 << k, 100 + 250 * k) for k in range(WIDTH.bit_length() - 1))
+CLOSE = 100 + 250 * len(MERGES)
+STAGES = tuple((WIDTH << k, CLOSE + 100 + 125 * k) for k in range((CHUNKS // WIDTH).bit_length() - 1))
+TILES = CLOSE + 100 + 125 * len(STAGES)
+VALUES = 15 + 10 * len(MERGES) + 5 * len(STAGES)
+
+
+def factor_kernel(
+    jac_hbm, step_hbm, src_hbm, flux_hbm, jac_ref, step_ref, src_ref, flux_ref, fac_ref, pack_ref, end_ref, sems
+):
+    needed = [pltpu.make_async_copy(jac_hbm.at[a, a:], jac_ref.at[a, a:], sems.at[a]) for a in N]
+    needed.append(pltpu.make_async_copy(step_hbm, step_ref, sems.at[5]))
+    later = [
+        pltpu.make_async_copy(src_hbm, src_ref, sems.at[6]),
+        pltpu.make_async_copy(flux_hbm, flux_ref, sems.at[7]),
+    ]
+    for copy in needed + later:
+        copy.start()
+    for copy in needed:
+        copy.wait()
+    factor(jac_ref, step_ref, fac_ref, pack_ref, end_ref)
+    for copy in later:
+        copy.wait()
+
+
+def factor(jac_ref, step_ref, fac_ref, pack_ref, end_ref):
     e = damping
     h0 = half_jacobian(jac_ref, 0)
     h1 = half_jacobian(jac_ref, 1)
@@ -256,9 +271,7 @@
     d2 = diagonal(step_ref, 2)
     h0p, h1p, h2p, h3p = shifted(h0, e), shifted(h1, e), shifted(h2, e), shifted(h3, e)
     h0m, h1m, h2m, h3m = shifted(h0, -e), shifted(h1, -e), shifted(h2, -e), shifted(h3, -e)
-    inv = inverse(shifted(mm(h2m, h1p), d1 * d2))
-    by_low = mm(inv, h0p)
-    by_upp = mm(inv, mm(h2m, h3m))
+    inv, by_low, by_upp = inverse_and_solved(shifted(mm(h2m, h1p), d1 * d2), h0p, mm(h2m, h3m))
     by_end = mm(flipped(inv), h3m)
     pair = mm(h2p, h1p)
     group = (
@@ -275,25 +288,33 @@
         latter = tuple(mturn(part, -distance) for part in group)
         group = merge(fac_ref, base, group, latter, mturn(h0m, -distance), mturn(h3p, 1 - distance))
     head_head, head_tail, tail_head, tail_tail = group
-    inv = inverse(head_head)
-    reach = mm(inv, head_tail)
+    inv, reach = inverse_and_solved(head_head, head_tail)
     through = mm(tail_head, inv)
     into = mm(h0m, inv)
     keep(fac_ref, CLOSE, inv)
     keep(fac_ref, CLOSE + 25, reach)
     keep(fac_ref, CLOSE + 50, through)
     keep(fac_ref, CLOSE + 75, into)
-    keep(end_ref, 0, through)
-    keep(end_ref, 25, minus(tail_tail, mm(tail_head, reach)))
-    keep(end_ref, 50, into)
-    keep(end_ref, 75, negative(mm(h0m, reach)))
+    own = minus(tail_tail, mm(tail_head, reach))
+    upp = mturn(negative(mm(h0m, reach)), -WIDTH)
+    low, nxt = through, into
+    if STAGES:
+        link = shifted(half_before(h3), e)
+        low, nxt = mm(through, link), mm(into, link)
+    nxt = mturn(nxt, -WIDTH)
+    for distance, base in STAGES:
+        low, own, nxt, upp = stage(fac_ref, base, low, own, nxt, upp, distance)
+    keep(end_ref, 0, low)
+    keep(end_ref, 25, own)
+    keep(end_ref, 50, nxt)
+    keep(end_ref, 75, upp)
     place = 100
     for a in N:
         for b in range(a, 5):
-            end_ref[8 * place : 8 * place + 8, :] = turn(h3p[a][b], 1)
+            end_ref[8 * place : 8 * place + 8, :] = turn(h3p[a][b], 1 - WIDTH)
             place += 1
     for number in range(15):
-        pack_ref[8 * number : 8 * number + 8, :] = rows_of_first(end_ref, number)
+        pack_ref[8 * number : 8 * number + 8, :] = rows_of_last(end_ref, number)
 
 
 def rhs_kernel(
@@ -327,16 +348,31 @@
         keep_vector(val_ref, place + 5, inner_head)
         place += 10
     keep_vector(val_ref, place, mv(block(fac_ref, CLOSE), head))
+    own = vminus(tail, mv(block(fac_ref, CLOSE + 50), head))
+    nxt = vturn([-value for value in mv(block(fac_ref, CLOSE + 75), head)], -WIDTH)
+    for distance, base in STAGES:
+        place += 5
+        value, own, nxt = stage_rhs(fac_ref, base, own, nxt, distance)
+        keep_vector(val_ref, place, value)
     end_ref[...] = jnp.zeros_like(end_ref)
-    keep_vector(end_ref, 3, vminus(tail, mv(block(fac_ref, CLOSE + 50), head)))
-    keep_vector(end_ref, 8, [-value for value in mv(block(fac_ref, CLOSE + 75), head)])
+    keep_vector(end_ref, 3, own)
+    keep_vector(end_ref, 8, nxt)
     pack_ref[:112, :] = part_ref[:112, :]
     row = lax.broadcasted_iota(jnp.int32, (8, LANES), 0)
-    pack_ref[112:120, :] = jnp.where(row < 3, part_ref[112:120, :], rows_of_first(end_ref, 0))
-    pack_ref[120:125, :] = rows_of_first(end_ref, 1)[:5]
-
-
-def solve_kernel(sent_ref, jac_ref, step_ref, fac_ref, val_ref, out_ref, all_ref, red_ref, x_ref, w_ref):
+    pack_ref[112:120, :] = jnp.where(row < 3, part_ref[112:120, :], rows_of_last(end_ref, 0))
+    pack_ref[120:125, :] = rows_of_last(end_ref, 1)[:5]
+
+
+def solve_kernel(sent_ref, jac_ref, step_ref, fac_ref, val_ref, out_hbm, out_ref, all_ref, red_ref, x_ref, w_ref, sems):
+    solve(sent_ref, jac_ref, step_ref, fac_ref, val_ref, out_ref, all_ref, red_ref, x_ref, w_ref)
+    copies = [pltpu.make_async_copy(out_ref.at[a], out_hbm.at[a], sems.at[a]) for a in N]
+    for copy in copies:
+        copy.start()
+    for copy in copies:
+        copy.wait()
+
+
+def solve(sent_ref, jac_ref, step_ref, fac_ref, val_ref, out_ref, all_ref, red_ref, x_ref, w_ref):
     e = damping
     for device in range(16):
         all_ref[ROWS * device : ROWS * device + SENT, :] = sent_ref[device]
@@ -361,9 +397,9 @@
 
     m_even = packed_symmetric(0, 100)
     m_odd = packed_symmetric(1, 100)
-    inv = inverse(plus(packed_block(0, 25), mm(packed_block(1, 50), m_even)))
-    vlow = mm(inv, packed_block(0, 0))
-    vupp = mm(inv, packed_block(1, 75))
+    inv, vlow, vupp = inverse_and_solved(
+        plus(packed_block(0, 25), mm(packed_block(1, 50), m_even)), packed_block(0, 0), packed_block(1, 75)
+    )
     value = mv(inv, vplus(packed_vector(0, 115), packed_vector(1, 120)))
     keep(red_ref, VLOW, vlow)
     keep(red_ref, VUPP, vupp)
@@ -407,12 +443,24 @@
     ends = [jnp.broadcast_to(x_ref[pl.ds(8 * a + half, 1), :], (CHUNKS, LANES)) for a in N]
     w = [jnp.broadcast_to(w_ref[pl.ds(8 * a + half, 1), :], (CHUNKS, LANES)) for a in N]
 
+    def neighbour(values, distance):
+        return [jnp.where(row < distance, w[a], turn(values[a], distance)) for a in N]
+
     last = ends
-    first = vplus(vector(val_ref, 40), vminus(mv(block(fac_ref, CLOSE), w), mv(block(fac_ref, CLOSE + 25), last)))
-    place = 30
+    place = VALUES - 5
+    for distance, base in reversed(STAGES):
+        found = stage_back(fac_ref, base, vector(val_ref, place), neighbour(last, distance), vturn(last, -distance))
+        place -= 5
+        chosen = (row % (2 * distance)) == distance - WIDTH
+        last = [jnp.where(chosen, found[a], last[a]) for a in N]
+    if STAGES:
+        w = mv(shifted(half_before(half_jacobian(jac_ref, 3)), e), neighbour(last, WIDTH))
+    first = vplus(
+        vector(val_ref, place), vminus(mv(block(fac_ref, CLOSE), w), mv(block(fac_ref, CLOSE + 25), last))
+    )
     for distance, base in reversed(MERGES):
+        place -= 10
         tail, head = merge_back(fac_ref, base, vector(val_ref, place), vector(val_ref, place + 5), first, last)
-        place -= 10
         latter = (row % (2 * distance)) >= distance
         first = [jnp.where(latter, turn(head[a], distance), first[a]) for a in N]
         last = [jnp.where(latter, turn(last[a], distance), tail[a]) for a in N]
@@ -433,46 +481,81 @@
 INTERPRET = False
 
 
-def run(kernel, name, outs, args, scratch):
-    inside = pl.BlockSpec(memory_space=pltpu.VMEM)
-    if INTERPRET:
-        shapes = [jax.ShapeDtypeStruct(shape, jnp.float32) for shape in outs]
-    else:
-        args = [pltpu.with_memory_space_constraint(arg, pltpu.VMEM) for arg in args]
-        shapes = [pltpu.VMEM(shape, jnp.float32) for shape in outs]
+VMEM = pl.BlockSpec(memory_space=pltpu.VMEM)
+HBM = pl.BlockSpec(memory_space=pltpu.MemorySpace.HBM)
+
+
+def kept(shape, dtype=jnp.float32):
+    return jax.ShapeDtypeStruct(shape, dtype) if INTERPRET else pltpu.VMEM(shape, dtype)
+
+
+def inside(values):
+    return values if INTERPRET else [pltpu.with_memory_space_constraint(value, pltpu.VMEM) for value in values]
+
+
+def outside(values):
+    return values if INTERPRET else [pltpu.with_memory_space_constraint(value, pltpu.MemorySpace.HBM) for value in values]
+
+
+def run(kernel, name, outs, args, scratch, far_args=0, far_outs=0):
     return pl.pallas_call(
         kernel,
-        out_shape=shapes,
-        in_specs=[inside] * len(args),
-        out_specs=[inside] * len(outs),
-        scratch_shapes=[pltpu.VMEM(shape, jnp.float32) for shape in scratch],
+        out_shape=outs,
+        in_specs=[HBM] * far_args + [VMEM] * (len(args) - far_args),
+        out_specs=[HBM] * far_outs + [VMEM] * (len(outs) - far_outs),
+        scratch_shapes=scratch,
+        compiler_params=pltpu.CompilerParams(vmem_limit_bytes=12 << 20),
         interpret=INTERPRET,
-        compiler_params=pltpu.CompilerParams(vmem_limit_bytes=12 << 20),
         name=name,
-    )(*args)
+    )(*outside(args[:far_args]), *inside(args[far_args:]))
+
+
+def tiles(count):
+    return pltpu.VMEM((8 * count, LANES), jnp.float32)
 
 
 def shards(jacobian, time_step, source, cross_flux):
     count = lax.axis_size("cross")
+    cells = CHUNKS * CELLS
     before = lax.ppermute(cross_flux, "cross", [(i, i + 1) for i in range(count - 1)])
     after = lax.ppermute(cross_flux, "cross", [(i + 1, i) for i in range(count - 1)])
-    factors, part = run(
-        factor_kernel, "factor", [(TILES * 8, LANES), (120, LANES)], [jacobian, time_step], [(120 * 8, LANES)]
+    jac, step, src, flux, factors, part = run(
+        factor_kernel,
+        "factor",
+        [
+            kept((5, 5, cells, LANES)),
+            kept((cells, LANES)),
+            kept((5, cells, LANES), jnp.bfloat16),
+            kept((5, cells, LANES), jnp.bfloat16),
+            kept((8 * TILES, LANES)),
+            kept((120, LANES)),
+        ],
+        [jacobian, time_step, source, cross_flux],
+        [tiles(120), pltpu.SemaphoreType.DMA((8,))],
+        far_args=4,
     )
     packet, values = run(
         rhs_kernel,
         "right_side",
-        [(SENT, LANES), (45 * 8, LANES)],
-        [jacobian, time_step, source, cross_flux, before, after, factors, part],
-        [(5, CHUNKS * CELLS, LANES), (16 * 8, LANES)],
+        [kept((SENT, LANES)), kept((8 * VALUES, LANES))],
+        [jac, step, src, flux, before, after, factors, part],
+        [pltpu.VMEM((5, cells, LANES), jnp.float32), tiles(16)],
     )
     packets = lax.all_gather(packet, "line", axis=0)
     return run(
         solve_kernel,
         "solve",
-        [(5, CHUNKS * CELLS, LANES)],
-        [packets, jacobian, time_step, factors, values],
-        [(16 * ROWS, LANES), (4 * STAGE * 8, LANES), (16 * 8, LANES), (5 * 8, LANES)],
+        [jax.ShapeDtypeStruct((5, cells, LANES), jnp.float32)],
+        [packets, jac, step, factors, values],
+        [
+            pltpu.VMEM((5, cells, LANES), jnp.float32),
+            tiles(2 * ROWS),
+            tiles(4 * STAGE),
+            tiles(16),
+            tiles(5),
+            pltpu.SemaphoreType.DMA((5,)),
+        ],
+        far_outs=1,
     )[0]
 
 

time: 41.4 us -> 37.3 us (0.901)
  the two profiles are of different devices: /device:TPU:199 before, /device:TPU:257 now
where the time goes in v1:
time: 37.3 us; the launch traced here: 37.1 us
  blocking collectives  22.5 us (60%)
  Pallas kernels  5.71 us (15%)
  starting transfers between devices  5.38 us (14%)
  waiting for transfers between devices  3.51 us (9%)
    all_gather x1, blocking collectives, shards(): packets = lax.all_gather(packet, 'line', axis=0)  22.5 us
    pallas_call x3, Pallas kernels, run(): pl.pallas_call(kernel, out_shape=outs, in_specs=[HBM] * far_args + [VMEM]...  5.71 us
    ppermute x1, waiting for transfers between devices, shards(): lax.ppermute(cross_flux, 'cross', [(i, i + 1) for i in range(count - 1)])  3.5 us
    ppermute x1, starting transfers between devices, shards(): lax.ppermute(cross_flux, 'cross', [(i + 1, i) for i in range(count - 1)])  3.46 us
    ppermute x1, starting transfers between devices, shards(): lax.ppermute(cross_flux, 'cross', [(i, i + 1) for i in range(count - 1)])  1.92 us
  transfers between devices with their start and end apart: 2, of which 1 were waited for; matrix products, arithmetic and copies ran while one was open for 0% of the time, Pallas kernels for 8%

profile of v1, /device:TPU:257, one launch (start us, length us, event | category | flops | bytes accessed | tf_op | source)
XLA Modules:
  0.0 37.1 jit_solution(11698352821550950723)
XLA Ops:
  0.0 3.5 %collective-permute-start.1 = (bf16[5,32,128]{2,1,0:T(8,128)(2,1)}, bf16[5,32,128]{2,1,0:T(8,128)(2,1)S(1)}, u32[]{:S(2)}, u32[]{:S(2)}) collective-permute-start(bf16[5,32,128]{2,1,0:T(8,128)(2,1)} %flux_hbm.1), channel_id=1, source_target_pairs={{1,0},{2,1},{3,2},{4,3},{5,4},{6,5},{7,6},{8,7},{9,8},{10,9},{11,1... | collective-permute-start | bytes 122888 | tf_op jit(solution)/shard_map/ppermute | solution.py:521
  3.5 1.9 %collective-permute-start = (bf16[5,32,128]{2,1,0:T(8,128)(2,1)}, bf16[5,32,128]{2,1,0:T(8,128)(2,1)S(1)}, u32[]{:S(2)}, u32[]{:S(2)}) collective-permute-start(bf16[5,32,128]{2,1,0:T(8,128)(2,1)} %flux_hbm.1), channel_id=1, source_target_pairs={{0,1},{1,2},{2,3},{3,4},{4,5},{5,6},{6,7},{7,8},{8,9},{9,10},{10,1... | collective-permute-start | bytes 122888 | tf_op jit(solution)/shard_map/ppermute | solution.py:520
  5.4 2.8 %factor.1 = (f32[5,5,32,128]{3,2,1,0:T(8,128)S(1)}, f32[32,128]{1,0:T(8,128)S(1)}, bf16[5,32,128]{2,1,0:T(8,128)(2,1)S(1)}, bf16[5,32,128]{2,1,0:T(8,128)(2,1)S(...) custom-call(f32[5,5,32,128]{3,2,1,0:T(8,128)} %jac_hbm.1, f32[32,128]{1,0:T(8,128)} %step_hbm.1, ...), custom_call_target="tpu_custom_call" | custom-call | tf_op jit(solution)/shard_map/factor/pallas_call | solution.py:501
  8.2 0.0 collective-permute-done.1.after_ref
  8.2 3.5 %collective-permute-done.before_ref = bf16[5,32,128]{2,1,0:T(8,128)(2,1)S(1)} collective-permute-done((bf16[5,32,128]{2,1,0:T(8,128)(2,1)}, bf16[5,32,128]{2,1,0:T(8,128)(2,1)S(1)}, u32[]{:S(2)}, u32[]{:S(2)}) %collective-permute-start) | collective-permute-done | bytes 40992 | tf_op jit(solution)/shard_map/ppermute | solution.py:520
  11.7 0.3 right_side.1
  12.0 22.5 %all-gather.1.sent_ref = f32[16,125,128]{2,1,0:T(8,128)S(1)} all-gather(f32[1,125,128]{2,1,0:T(8,128)S(1)} %bitcast.1), channel_id=2, replica_groups=mesh['line'=16,'cross'=32] {'line'}, dimensions={0}, use_global_device_ids=true | all-gather | bytes 1088000 | tf_op jit(solution)/shard_map/all_gather | solution.py:544
  34.5 2.6 %solve.1 = f32[5,32,128]{2,1,0:T(8,128)} custom-call(f32[16,125,128]{2,1,0:T(8,128)S(1)} %all-gather.1.sent_ref, f32[5,5,32,128]{3,2,1,0:T(8,128)S(1)} %get-tuple-element.13.jac_ref, f32[32,128]{1,0:T(8,128)S(1)} %get-tuple-element.14.step_ref, f32[5600,128]{1,0:T(8,128)S(1)} %get-tuple-element.17.fac_ref, f32[280,128]{1,0:T(8,128)S(1)} %get-tuple-element.20.val_ref), custom_call_target="tpu_custom_call" | custom-call | tf_op jit(solution)/shard_map/solve/pallas_call | solution.py:501
Async XLA Ops:
  0.0 8.2 %collective-permute-start.1 = (bf16[5,32,128]{2,1,0:T(8,128)(2,1)}, bf16[5,32,128]{2,1,0:T(8,128)(2,1)S(1)}, u32[]{:S(2)}, u32[]{:S(2)}) collective-permute-start(bf16[5,32,128]{2,1,0:T(8,128)(2,1)} %flux_hbm.1), channel_id=1, source_target_pairs={{1,0},{2,1},{3,2},{4,3},{5,4},{6,5},{7,6},{8,7},{9,8},{10,9},{11,1... | collective-permute-start | bytes 122888 | tf_op jit(solution)/shard_map/ppermute | solution.py:521
  3.5 8.3 %collective-permute-start = (bf16[5,32,128]{2,1,0:T(8,128)(2,1)}, bf16[5,32,128]{2,1,0:T(8,128)(2,1)S(1)}, u32[]{:S(2)}, u32[]{:S(2)}) collective-permute-start(bf16[5,32,128]{2,1,0:T(8,128)(2,1)} %flux_hbm.1), channel_id=1, source_target_pairs={{0,1},{1,2},{2,3},{3,4},{4,5},{5,6},{6,7},{7,8},{8,9},{9,10},{10,1... | collective-permute-start | bytes 122888 | tf_op jit(solution)/shard_map/ppermute | solution.py:520

commit v2 on v1

--- a/solution.py
+++ b/solution.py
@@ -318,14 +318,19 @@
 
 
 def rhs_kernel(
-    jac_ref, step_ref, src_ref, flux_ref, before_ref, after_ref, fac_ref, part_ref, pack_ref, val_ref, res_ref, end_ref
+    jac_ref, step_ref, src_ref, flux_ref, even_ref, odd_ref, fac_ref, part_ref, pack_ref, val_ref, res_ref, end_ref
 ):
     e = damping
     lane = lax.broadcasted_iota(jnp.int32, (CHUNKS * CELLS, LANES), 1)
+    is_even = lax.axis_index("cross") % 2 == 0
     for a in N:
         flux = flux_ref[a].astype(jnp.float32)
-        upper = pltpu.roll(jnp.where(lane < NZ, after_ref[a].astype(jnp.float32), flux), LANES - NZ, axis=1)
-        lower = pltpu.roll(jnp.where(lane >= LANES - NZ, before_ref[a].astype(jnp.float32), flux), NZ, axis=1)
+        even_swap = even_ref[a].astype(jnp.float32)
+        odd_swap = odd_ref[a].astype(jnp.float32)
+        after = jnp.where(is_even, even_swap, odd_swap)
+        before = jnp.where(is_even, odd_swap, even_swap)
+        upper = pltpu.roll(jnp.where(lane < NZ, after, flux), LANES - NZ, axis=1)
+        lower = pltpu.roll(jnp.where(lane >= LANES - NZ, before, flux), NZ, axis=1)
         res_ref[a] = src_ref[a].astype(jnp.float32) - 0.5 * (upper - lower)
     r0, r1, r2, r3 = ([res_ref[a, pl.ds(cell, CHUNKS, stride=CELLS), :] for a in N] for cell in range(CELLS))
     h1 = half_jacobian(jac_ref, 1)
@@ -517,8 +522,14 @@
 def shards(jacobian, time_step, source, cross_flux):
     count = lax.axis_size("cross")
     cells = CHUNKS * CELLS
-    before = lax.ppermute(cross_flux, "cross", [(i, i + 1) for i in range(count - 1)])
-    after = lax.ppermute(cross_flux, "cross", [(i + 1, i) for i in range(count - 1)])
+    even_swap, odd_swap = (
+        lax.ppermute(
+            cross_flux,
+            "cross",
+            [pair for i in range(start, count - 1, 2) for pair in ((i, i + 1), (i + 1, i))],
+        )
+        for start in (0, 1)
+    )
     jac, step, src, flux, factors, part = run(
         factor_kernel,
         "factor",
@@ -538,7 +549,7 @@
         rhs_kernel,
         "right_side",
         [kept((SENT, LANES)), kept((8 * VALUES, LANES))],
-        [jac, step, src, flux, before, after, factors, part],
+        [jac, step, src, flux, even_swap, odd_swap, factors, part],
         [pltpu.VMEM((5, cells, LANES), jnp.float32), tiles(16)],
     )
     packets = lax.all_gather(packet, "line", axis=0)

time: 37.3 us -> 35.6 us (0.954)
  the two profiles are of different devices: /device:TPU:257 before, /device:TPU:199 now
where the time goes in v2:
time: 35.6 us; the launch traced here: 35.5 us
  blocking collectives  22.5 us (63%)
  starting transfers between devices  7.03 us (20%)
  Pallas kernels  5.72 us (16%)
    all_gather x1, blocking collectives, shards(): packets = lax.all_gather(packet, 'line', axis=0)  22.5 us
    ppermute x2, starting transfers between devices, shards(): lax.ppermute(cross_flux, 'cross', [pair for i in range(start, count - 1,...  7.03 us
    pallas_call x3, Pallas kernels, run(): pl.pallas_call(kernel, out_shape=outs, in_specs=[HBM] * far_args + [VMEM]...  5.72 us
  transfers between devices with their start and end apart: 2, of which 1 were waited for; matrix products, arithmetic and copies ran while one was open for 0% of the time, Pallas kernels for 8%

profile of v2, /device:TPU:199, one launch (start us, length us, event | category | flops | bytes accessed | tf_op | source)
XLA Modules:
  0.0 35.5 jit_solution(13463030973614716481)
XLA Ops:
  0.0 5.1 %collective-permute-start.1 = (bf16[5,32,128]{2,1,0:T(8,128)(2,1)}, bf16[5,32,128]{2,1,0:T(8,128)(2,1)S(1)}, u32[]{:S(2)}, u32[]{:S(2)}) collective-permute-start(bf16[5,32,128]{2,1,0:T(8,128)(2,1)} %flux_hbm.1), channel_id=1, source_target_pairs={{1,2},{2,1},{3,4},{4,3},{5,6},{6,5},{7,8},{8,7},{9,10},{10,9},{11,... | collective-permute-start | bytes 122888 | tf_op jit(solution)/shard_map/ppermute | solution.py:526
  5.1 1.9 %collective-permute-start = (bf16[5,32,128]{2,1,0:T(8,128)(2,1)}, bf16[5,32,128]{2,1,0:T(8,128)(2,1)S(1)}, u32[]{:S(2)}, u32[]{:S(2)}) collective-permute-start(bf16[5,32,128]{2,1,0:T(8,128)(2,1)} %flux_hbm.1), channel_id=1, source_target_pairs={{0,1},{1,0},{2,3},{3,2},{4,5},{5,4},{6,7},{7,6},{8,9},{9,8},{10,11... | collective-permute-start | bytes 122888 | tf_op jit(solution)/shard_map/ppermute | solution.py:526
  7.0 2.8 %factor.1 = (f32[5,5,32,128]{3,2,1,0:T(8,128)S(1)}, f32[32,128]{1,0:T(8,128)S(1)}, bf16[5,32,128]{2,1,0:T(8,128)(2,1)S(1)}, bf16[5,32,128]{2,1,0:T(8,128)(2,1)S(...) custom-call(f32[5,5,32,128]{3,2,1,0:T(8,128)} %jac_hbm.1, f32[32,128]{1,0:T(8,128)} %step_hbm.1, ...), custom_call_target="tpu_custom_call" | custom-call | tf_op jit(solution)/shard_map/factor/pallas_call | solution.py:506
  9.9 0.0 collective-permute-done.1.odd_ref
  9.9 0.2 collective-permute-done.even_ref
  10.1 0.3 right_side.1
  10.4 22.5 %all-gather.1.sent_ref = f32[16,125,128]{2,1,0:T(8,128)S(1)} all-gather(f32[1,125,128]{2,1,0:T(8,128)S(1)} %bitcast.1), channel_id=2, replica_groups=mesh['line'=16,'cross'=32] {'line'}, dimensions={0}, use_global_device_ids=true | all-gather | bytes 1088000 | tf_op jit(solution)/shard_map/all_gather | solution.py:555
  32.9 2.6 %solve.1 = f32[5,32,128]{2,1,0:T(8,128)} custom-call(f32[16,125,128]{2,1,0:T(8,128)S(1)} %all-gather.1.sent_ref, f32[5,5,32,128]{3,2,1,0:T(8,128)S(1)} %get-tuple-element.13.jac_ref, f32[32,128]{1,0:T(8,128)S(1)} %get-tuple-element.14.step_ref, f32[5600,128]{1,0:T(8,128)S(1)} %get-tuple-element.17.fac_ref, f32[280,128]{1,0:T(8,128)S(1)} %get-tuple-element.20.val_ref), custom_call_target="tpu_custom_call" | custom-call | tf_op jit(solution)/shard_map/solve/pallas_call | solution.py:506
Async XLA Ops:
  0.0 9.9 %collective-permute-start.1 = (bf16[5,32,128]{2,1,0:T(8,128)(2,1)}, bf16[5,32,128]{2,1,0:T(8,128)(2,1)S(1)}, u32[]{:S(2)}, u32[]{:S(2)}) collective-permute-start(bf16[5,32,128]{2,1,0:T(8,128)(2,1)} %flux_hbm.1), channel_id=1, source_target_pairs={{1,2},{2,1},{3,4},{4,3},{5,6},{6,5},{7,8},{8,7},{9,10},{10,9},{11,... | collective-permute-start | bytes 122888 | tf_op jit(solution)/shard_map/ppermute | solution.py:526
  5.1 5.0 %collective-permute-start = (bf16[5,32,128]{2,1,0:T(8,128)(2,1)}, bf16[5,32,128]{2,1,0:T(8,128)(2,1)S(1)}, u32[]{:S(2)}, u32[]{:S(2)}) collective-permute-start(bf16[5,32,128]{2,1,0:T(8,128)(2,1)} %flux_hbm.1), channel_id=1, source_target_pairs={{0,1},{1,0},{2,3},{3,2},{4,5},{5,4},{6,7},{7,6},{8,9},{9,8},{10,11... | collective-permute-start | bytes 122888 | tf_op jit(solution)/shard_map/ppermute | solution.py:526

commit v3 on v2

--- a/solution.py
+++ b/solution.py
@@ -98,20 +98,6 @@
 
 def vturn(values, count):
     return [turn(values[a], count) for a in N]
-
-
-def inverse(matrix):
-    m = [list(row) for row in matrix]
-    for k in N:
-        pivot = 1.0 / m[k][k]
-        for b in N:
-            m[k][b] = pivot if b == k else m[k][b] * pivot
-        for a in N:
-            if a != k:
-                factor = m[a][k]
-                for b in N:
-                    m[a][b] = -factor * pivot if b == k else m[a][b] - factor * m[k][b]
-    return m
 
 
 def inverse_and_solved(matrix, *sides):
@@ -129,6 +115,20 @@
     return [[row[at : at + 5] for row in m] for at in range(0, width, 5)]
 
 
+def solved(matrix, values, *sides):
+    m = [list(row) + [values[a]] + [side[a][b] for side in sides for b in N] for a, row in enumerate(matrix)]
+    width = len(m[0])
+    for k in N:
+        pivot = 1.0 / m[k][k]
+        for b in range(k + 1, width):
+            m[k][b] = m[k][b] * pivot
+        for a in N:
+            if a != k:
+                for b in range(k + 1, width):
+                    m[a][b] = m[a][b] - m[a][k] * m[k][b]
+    return [row[5] for row in m], [[row[at : at + 5] for row in m] for at in range(6, width, 5)]
+
+
 def half_jacobian(jac_ref, cell):
     half = [[None] * 5 for _ in N]
     for a in N:
@@ -149,6 +149,19 @@
 
 def diagonal(step_ref, cell):
     return 1.0 / step_ref[pl.ds(cell, CHUNKS, stride=CELLS), :] + 2.0 * damping
+
+
+def next_rows(low, own, nxt, upp, vlow, vupp, distance):
+    vlow_before, vupp_before = mturn(vlow, distance), mturn(vupp, distance)
+    vlow_after, vupp_after = vlow_before, vupp_before
+    if 2 * distance != CHUNKS:
+        vlow_after, vupp_after = mturn(vlow, -distance), mturn(vupp, -distance)
+    return (
+        negative(mm(low, vlow_before)),
+        minus(own, mm(low, vupp_before)),
+        minus(nxt, mm(upp, vlow_after)),
+        negative(mm(upp, vupp_after)),
+    )
 
 
 def stage(fac_ref, base, low, own, nxt, upp, distance):
@@ -158,11 +171,7 @@
     keep(fac_ref, base + UPP, upp)
     keep(fac_ref, base + VLOW, vlow)
     keep(fac_ref, base + VUPP, vupp)
-    own = minus(own, mm(low, mturn(vupp, distance)))
-    nxt = minus(nxt, mm(upp, mturn(vlow, -distance)))
-    low = negative(mm(low, mturn(vlow, distance)))
-    upp = negative(mm(upp, mturn(vupp, -distance)))
-    return low, own, nxt, upp
+    return next_rows(low, own, nxt, upp, vlow, vupp, distance)
 
 
 def stage_rhs(fac_ref, base, own, nxt, distance):
@@ -402,10 +411,12 @@
 
     m_even = packed_symmetric(0, 100)
     m_odd = packed_symmetric(1, 100)
-    inv, vlow, vupp = inverse_and_solved(
-        plus(packed_block(0, 25), mm(packed_block(1, 50), m_even)), packed_block(0, 0), packed_block(1, 75)
-    )
-    value = mv(inv, vplus(packed_vector(0, 115), packed_vector(1, 120)))
+    value, (vlow, vupp) = solved(
+        plus(packed_block(0, 25), mm(packed_block(1, 50), m_even)),
+        vplus(packed_vector(0, 115), packed_vector(1, 120)),
+        packed_block(0, 0),
+        packed_block(1, 75),
+    )
     keep(red_ref, VLOW, vlow)
     keep(red_ref, VUPP, vupp)
     keep_vector(x_ref, 4, value)
@@ -424,17 +435,12 @@
     nxt = [[jnp.where(last, 0.0, nxt[a][b]) for b in N] for a in N]
     upp = [[jnp.where(last, 0.0, turn(upp[a][b], -1)) for b in N] for a in N]
     nxt_rhs = [jnp.where(last, 0.0, turn(nxt_rhs[a], -1)) for a in N]
-    levels = ((1, 1), (2, 2), (3, 4))
-    values = []
-    for number, distance in levels:
-        low, own, nxt, upp = stage(red_ref, number * STAGE, low, own, nxt, upp, distance)
-        value, own_rhs, nxt_rhs = stage_rhs(red_ref, number * STAGE, own_rhs, nxt_rhs, distance)
-        values.append(value)
-    x = mv(inverse(plus(own, nxt)), vplus(own_rhs, nxt_rhs))
-    for number, distance in reversed(levels):
-        found = stage_back(red_ref, number * STAGE, values[number - 1], vturn(x, distance), vturn(x, -distance))
-        chosen = (row % (2 * distance)) == distance - 1
-        x = [jnp.where(chosen, found[a], x[a]) for a in N]
+    for distance in (1, 2, 4):
+        value, (vlow, vupp) = solved(plus(own, nxt), vplus(own_rhs, nxt_rhs), low, upp)
+        own_rhs = vminus(own_rhs, mv(low, vturn(value, distance)))
+        nxt_rhs = vminus(nxt_rhs, mv(upp, vturn(value, -distance)))
+        low, own, nxt, upp = next_rows(low, own, nxt, upp, vlow, vupp, distance)
+    x = solved(plus(own, nxt), vplus(own_rhs, nxt_rhs))[0]
     w_odd = mv(m_odd, x)
     before = [jnp.where(first, 0.0, turn(w_odd[a], 1)) for a in N]
     x_even = stage_back(red_ref, 0, vector(x_ref, 4), before, x)
@@ -561,7 +567,7 @@
         [
             pltpu.VMEM((5, cells, LANES), jnp.float32),
             tiles(2 * ROWS),
-            tiles(4 * STAGE),
+            tiles(STAGE),
             tiles(16),
             tiles(5),
             pltpu.SemaphoreType.DMA((5,)),

time: 35.6 us -> 35.5 us (level)
  no operation moved by 1% of the time
where the time goes in v3:
time: 35.5 us; the launch traced here: 35.3 us
  blocking collectives  22.5 us (63%)
  starting transfers between devices  7.03 us (20%)
  Pallas kernels  5.6 us (16%)
    all_gather x1, blocking collectives, shards(): packets = lax.all_gather(packet, 'line', axis=0)  22.5 us
    ppermute x2, starting transfers between devices, shards(): lax.ppermute(cross_flux, 'cross', [pair for i in range(start, count - 1,...  7.03 us
    pallas_call x3, Pallas kernels, run(): pl.pallas_call(kernel, out_shape=outs, in_specs=[HBM] * far_args + [VMEM]...  5.6 us
  transfers between devices with their start and end apart: 2, of which 1 were waited for; matrix products, arithmetic and copies ran while one was open for 0% of the time, Pallas kernels for 8%

profile of v3, /device:TPU:199, one launch (start us, length us, event | category | flops | bytes accessed | tf_op | source)
XLA Modules:
  0.0 35.3 jit_solution(18166617987137206346)
XLA Ops:
  0.0 5.1 %collective-permute-start.1 = (bf16[5,32,128]{2,1,0:T(8,128)(2,1)}, bf16[5,32,128]{2,1,0:T(8,128)(2,1)S(1)}, u32[]{:S(2)}, u32[]{:S(2)}) collective-permute-start(bf16[5,32,128]{2,1,0:T(8,128)(2,1)} %flux_hbm.1), channel_id=1, source_target_pairs={{1,2},{2,1},{3,4},{4,3},{5,6},{6,5},{7,8},{8,7},{9,10},{10,9},{11,... | collective-permute-start | bytes 122888 | tf_op jit(solution)/shard_map/ppermute | solution.py:532
  5.1 1.9 %collective-permute-start = (bf16[5,32,128]{2,1,0:T(8,128)(2,1)}, bf16[5,32,128]{2,1,0:T(8,128)(2,1)S(1)}, u32[]{:S(2)}, u32[]{:S(2)}) collective-permute-start(bf16[5,32,128]{2,1,0:T(8,128)(2,1)} %flux_hbm.1), channel_id=1, source_target_pairs={{0,1},{1,0},{2,3},{3,2},{4,5},{5,4},{6,7},{7,6},{8,9},{9,8},{10,11... | collective-permute-start | bytes 122888 | tf_op jit(solution)/shard_map/ppermute | solution.py:532
  7.0 2.8 %factor.1 = (f32[5,5,32,128]{3,2,1,0:T(8,128)S(1)}, f32[32,128]{1,0:T(8,128)S(1)}, bf16[5,32,128]{2,1,0:T(8,128)(2,1)S(1)}, bf16[5,32,128]{2,1,0:T(8,128)(2,1)S(...) custom-call(f32[5,5,32,128]{3,2,1,0:T(8,128)} %jac_hbm.1, f32[32,128]{1,0:T(8,128)} %step_hbm.1, ...), custom_call_target="tpu_custom_call" | custom-call | tf_op jit(solution)/shard_map/factor/pallas_call | solution.py:512
  9.9 0.0 collective-permute-done.1.odd_ref
  9.9 0.2 collective-permute-done.even_ref
  10.1 0.3 right_side.1
  10.4 22.5 %all-gather.1.sent_ref = f32[16,125,128]{2,1,0:T(8,128)S(1)} all-gather(f32[1,125,128]{2,1,0:T(8,128)S(1)} %bitcast.1), channel_id=2, replica_groups=mesh['line'=16,'cross'=32] {'line'}, dimensions={0}, use_global_device_ids=true | all-gather | bytes 1088000 | tf_op jit(solution)/shard_map/all_gather | solution.py:561
  32.9 2.5 %solve.1 = f32[5,32,128]{2,1,0:T(8,128)} custom-call(f32[16,125,128]{2,1,0:T(8,128)S(1)} %all-gather.1.sent_ref, f32[5,5,32,128]{3,2,1,0:T(8,128)S(1)} %get-tuple-element.13.jac_ref, f32[32,128]{1,0:T(8,128)S(1)} %get-tuple-element.14.step_ref, f32[5600,128]{1,0:T(8,128)S(1)} %get-tuple-element.17.fac_ref, f32[280,128]{1,0:T(8,128)S(1)} %get-tuple-element.20.val_ref), custom_call_target="tpu_custom_call" | custom-call | tf_op jit(solution)/shard_map/solve/pallas_call | solution.py:512
Async XLA Ops:
  0.0 9.9 %collective-permute-start.1 = (bf16[5,32,128]{2,1,0:T(8,128)(2,1)}, bf16[5,32,128]{2,1,0:T(8,128)(2,1)S(1)}, u32[]{:S(2)}, u32[]{:S(2)}) collective-permute-start(bf16[5,32,128]{2,1,0:T(8,128)(2,1)} %flux_hbm.1), channel_id=1, source_target_pairs={{1,2},{2,1},{3,4},{4,3},{5,6},{6,5},{7,8},{8,7},{9,10},{10,9},{11,... | collective-permute-start | bytes 122888 | tf_op jit(solution)/shard_map/ppermute | solution.py:532
  5.1 5.0 %collective-permute-start = (bf16[5,32,128]{2,1,0:T(8,128)(2,1)}, bf16[5,32,128]{2,1,0:T(8,128)(2,1)S(1)}, u32[]{:S(2)}, u32[]{:S(2)}) collective-permute-start(bf16[5,32,128]{2,1,0:T(8,128)(2,1)} %flux_hbm.1), channel_id=1, source_target_pairs={{0,1},{1,0},{2,3},{3,2},{4,5},{5,4},{6,7},{7,6},{8,9},{9,8},{10,11... | collective-permute-start | bytes 122888 | tf_op jit(solution)/shard_map/ppermute | solution.py:532

commit v4 on v3

--- a/solution.py
+++ b/solution.py
@@ -377,16 +377,7 @@
     pack_ref[120:125, :] = rows_of_last(end_ref, 1)[:5]
 
 
-def solve_kernel(sent_ref, jac_ref, step_ref, fac_ref, val_ref, out_hbm, out_ref, all_ref, red_ref, x_ref, w_ref, sems):
-    solve(sent_ref, jac_ref, step_ref, fac_ref, val_ref, out_ref, all_ref, red_ref, x_ref, w_ref)
-    copies = [pltpu.make_async_copy(out_ref.at[a], out_hbm.at[a], sems.at[a]) for a in N]
-    for copy in copies:
-        copy.start()
-    for copy in copies:
-        copy.wait()
-
-
-def solve(sent_ref, jac_ref, step_ref, fac_ref, val_ref, out_ref, all_ref, red_ref, x_ref, w_ref):
+def solve_kernel(sent_ref, jac_ref, step_ref, fac_ref, val_ref, out_ref, all_ref, red_ref, x_ref, w_ref):
     e = damping
     for device in range(16):
         all_ref[ROWS * device : ROWS * device + SENT, :] = sent_ref[device]
@@ -562,17 +553,14 @@
     return run(
         solve_kernel,
         "solve",
-        [jax.ShapeDtypeStruct((5, cells, LANES), jnp.float32)],
+        [kept((5, cells, LANES))],
         [packets, jac, step, factors, values],
         [
-            pltpu.VMEM((5, cells, LANES), jnp.float32),
             tiles(2 * ROWS),
             tiles(STAGE),
             tiles(16),
             tiles(5),
-            pltpu.SemaphoreType.DMA((5,)),
         ],
-        far_outs=1,
     )[0]
 
 

time: 35.5 us -> 35.5 us (level)
  Pallas kernels: 5.6 us -> 4.93 us
  local copies, waits for them, and re-layouts: 0 us -> 0.64 us
    pallas_call x3, Pallas kernels: 5.6 us -> 4.93 us  [run(): pl.pallas_call(kernel, out_shape=outs, in_specs=[HBM] * far_args + [VMEM]...]
    unnamed x0 -> x1, local copies, waits for them, and re-layouts: none -> 0.64 us
where the time goes in v4:
time: 35.5 us; the launch traced here: 35.3 us
  blocking collectives  22.5 us (63%)
  starting transfers between devices  7.03 us (20%)
  Pallas kernels  4.93 us (14%)
  local copies, waits for them, and re-layouts  0.64 us (2%)
    all_gather x1, blocking collectives, shards(): packets = lax.all_gather(packet, 'line', axis=0)  22.5 us
    ppermute x2, starting transfers between devices, shards(): lax.ppermute(cross_flux, 'cross', [pair for i in range(start, count - 1,...  7.03 us
    pallas_call x3, Pallas kernels, run(): pl.pallas_call(kernel, out_shape=outs, in_specs=[HBM] * far_args + [VMEM]...  4.93 us
  transfers between devices with their start and end apart: 2, of which 1 were waited for; matrix products, arithmetic and copies ran while one was open for 0% of the time, Pallas kernels for 8%

profile of v4, /device:TPU:199, one launch (start us, length us, event | category | flops | bytes accessed | tf_op | source)
XLA Modules:
  0.0 35.3 jit_solution(3992806631851306530)
XLA Ops:
  0.0 5.1 %collective-permute-start.1 = (bf16[5,32,128]{2,1,0:T(8,128)(2,1)}, bf16[5,32,128]{2,1,0:T(8,128)(2,1)S(1)}, u32[]{:S(2)}, u32[]{:S(2)}) collective-permute-start(bf16[5,32,128]{2,1,0:T(8,128)(2,1)} %flux_hbm.1), channel_id=1, source_target_pairs={{1,2},{2,1},{3,4},{4,3},{5,6},{6,5},{7,8},{8,7},{9,10},{10,9},{11,... | collective-permute-start | bytes 122888 | tf_op jit(solution)/shard_map/ppermute | solution.py:523
  5.1 1.9 %collective-permute-start = (bf16[5,32,128]{2,1,0:T(8,128)(2,1)}, bf16[5,32,128]{2,1,0:T(8,128)(2,1)S(1)}, u32[]{:S(2)}, u32[]{:S(2)}) collective-permute-start(bf16[5,32,128]{2,1,0:T(8,128)(2,1)} %flux_hbm.1), channel_id=1, source_target_pairs={{0,1},{1,0},{2,3},{3,2},{4,5},{5,4},{6,7},{7,6},{8,9},{9,8},{10,11... | collective-permute-start | bytes 122888 | tf_op jit(solution)/shard_map/ppermute | solution.py:523
  7.0 2.8 %factor.1 = (f32[5,5,32,128]{3,2,1,0:T(8,128)S(1)}, f32[32,128]{1,0:T(8,128)S(1)}, bf16[5,32,128]{2,1,0:T(8,128)(2,1)S(1)}, bf16[5,32,128]{2,1,0:T(8,128)(2,1)S(...) custom-call(f32[5,5,32,128]{3,2,1,0:T(8,128)} %jac_hbm.1, f32[32,128]{1,0:T(8,128)} %step_hbm.1, ...), custom_call_target="tpu_custom_call" | custom-call | tf_op jit(solution)/shard_map/factor/pallas_call | solution.py:503
  9.9 0.0 collective-permute-done.1.odd_ref
  9.9 0.2 collective-permute-done.even_ref
  10.1 0.3 right_side.1
  10.4 22.5 %all-gather.1.sent_ref = f32[16,125,128]{2,1,0:T(8,128)S(1)} all-gather(f32[1,125,128]{2,1,0:T(8,128)S(1)} %bitcast.1), channel_id=2, replica_groups=mesh['line'=16,'cross'=32] {'line'}, dimensions={0}, use_global_device_ids=true | all-gather | bytes 1088000 | tf_op jit(solution)/shard_map/all_gather | solution.py:552
  32.9 1.8 %solve.1 = f32[5,32,128]{2,1,0:T(8,128)S(1)} custom-call(f32[16,125,128]{2,1,0:T(8,128)S(1)} %all-gather.1.sent_ref, f32[5,5,32,128]{3,2,1,0:T(8,128)S(1)} %get-tuple-element.13.jac_ref, f32[32,128]{1,0:T(8,128)S(1)} %get-tuple-element.14.step_ref, f32[5600,128]{1,0:T(8,128)S(1)} %get-tuple-element.17.fac_ref, f32[280,128]{1,0:T(8,128)S(1)} %get-tuple-element.20.val_ref), custom_call_target="tpu_custom_call" | custom-call | tf_op jit(solution)/shard_map/solve/pallas_call | solution.py:503
  34.7 0.6 %copy.5 = f32[5,32,128]{2,1,0:T(8,128)} copy(f32[5,32,128]{2,1,0:T(8,128)S(1)} %solve.1) | data formatting | bytes 163840
Async XLA Ops:
  0.0 9.9 %collective-permute-start.1 = (bf16[5,32,128]{2,1,0:T(8,128)(2,1)}, bf16[5,32,128]{2,1,0:T(8,128)(2,1)S(1)}, u32[]{:S(2)}, u32[]{:S(2)}) collective-permute-start(bf16[5,32,128]{2,1,0:T(8,128)(2,1)} %flux_hbm.1), channel_id=1, source_target_pairs={{1,2},{2,1},{3,4},{4,3},{5,6},{6,5},{7,8},{8,7},{9,10},{10,9},{11,... | collective-permute-start | bytes 122888 | tf_op jit(solution)/shard_map/ppermute | solution.py:523
  5.1 5.0 %collective-permute-start = (bf16[5,32,128]{2,1,0:T(8,128)(2,1)}, bf16[5,32,128]{2,1,0:T(8,128)(2,1)S(1)}, u32[]{:S(2)}, u32[]{:S(2)}) collective-permute-start(bf16[5,32,128]{2,1,0:T(8,128)(2,1)} %flux_hbm.1), channel_id=1, source_target_pairs={{0,1},{1,0},{2,3},{3,2},{4,5},{5,4},{6,7},{7,6},{8,9},{9,8},{10,11... | collective-permute-start | bytes 122888 | tf_op jit(solution)/shard_map/ppermute | solution.py:523

commit v5 on v4

--- a/solution.py
+++ b/solution.py
@@ -244,7 +244,7 @@
     return ref[pl.ds(64 * group + CHUNKS - WIDTH, 8, stride=8), :]
 
 
-WIDTH = 2
+WIDTH = 1
 MERGES = tuple((1 << k, 100 + 250 * k) for k in range(WIDTH.bit_length() - 1))
 CLOSE = 100 + 250 * len(MERGES)
 STAGES = tuple((WIDTH << k, CLOSE + 100 + 125 * k) for k in range((CHUNKS // WIDTH).bit_length() - 1))

time: 35.5 us -> 35.5 us (level)
  transfers between devices with their start and end apart: 2 -> 2, of which waited for: 1 -> 1; matrix products, arithmetic and copies ran while one was open for 0% -> 0% of each run, Pallas kernels for 8% -> 7%
where the time goes in v5:
time: 35.5 us; the launch traced here: 35.3 us
  blocking collectives  22.5 us (63%)
  starting transfers between devices  7.03 us (20%)
  Pallas kernels  4.64 us (13%)
  local copies, waits for them, and re-layouts  0.64 us (2%)
  waiting for transfers between devices  0.44 us (1%)
    all_gather x1, blocking collectives, shards(): packets = lax.all_gather(packet, 'line', axis=0)  22.5 us
    ppermute x2, starting transfers between devices, shards(): lax.ppermute(cross_flux, 'cross', [pair for i in range(start, count - 1,...  7.03 us
    pallas_call x3, Pallas kernels, run(): pl.pallas_call(kernel, out_shape=outs, in_specs=[HBM] * far_args + [VMEM]...  4.64 us
  transfers between devices with their start and end apart: 2, of which 1 were waited for; matrix products, arithmetic and copies ran while one was open for 0% of the time, Pallas kernels for 7%

profile of v5, /device:TPU:199, one launch (start us, length us, event | category | flops | bytes accessed | tf_op | source)
XLA Modules:
  0.0 35.3 jit_solution(9774611713896029300)
XLA Ops:
  0.0 5.1 %collective-permute-start.1 = (bf16[5,32,128]{2,1,0:T(8,128)(2,1)}, bf16[5,32,128]{2,1,0:T(8,128)(2,1)S(1)}, u32[]{:S(2)}, u32[]{:S(2)}) collective-permute-start(bf16[5,32,128]{2,1,0:T(8,128)(2,1)} %flux_hbm.1), channel_id=1, source_target_pairs={{1,2},{2,1},{3,4},{4,3},{5,6},{6,5},{7,8},{8,7},{9,10},{10,9},{11,... | collective-permute-start | bytes 122888 | tf_op jit(solution)/shard_map/ppermute | solution.py:523
  5.1 1.9 %collective-permute-start = (bf16[5,32,128]{2,1,0:T(8,128)(2,1)}, bf16[5,32,128]{2,1,0:T(8,128)(2,1)S(1)}, u32[]{:S(2)}, u32[]{:S(2)}) collective-permute-start(bf16[5,32,128]{2,1,0:T(8,128)(2,1)} %flux_hbm.1), channel_id=1, source_target_pairs={{0,1},{1,0},{2,3},{3,2},{4,5},{5,4},{6,7},{7,6},{8,9},{9,8},{10,11... | collective-permute-start | bytes 122888 | tf_op jit(solution)/shard_map/ppermute | solution.py:523
  7.0 2.6 %factor.1 = (f32[5,5,32,128]{3,2,1,0:T(8,128)S(1)}, f32[32,128]{1,0:T(8,128)S(1)}, bf16[5,32,128]{2,1,0:T(8,128)(2,1)S(1)}, bf16[5,32,128]{2,1,0:T(8,128)(2,1)S(...) custom-call(f32[5,5,32,128]{3,2,1,0:T(8,128)} %jac_hbm.1, f32[32,128]{1,0:T(8,128)} %step_hbm.1, ...), custom_call_target="tpu_custom_call" | custom-call | tf_op jit(solution)/shard_map/factor/pallas_call | solution.py:503
  9.6 0.0 collective-permute-done.1.odd_ref
  9.6 0.4 %collective-permute-done.even_ref = bf16[5,32,128]{2,1,0:T(8,128)(2,1)S(1)} collective-permute-done((bf16[5,32,128]{2,1,0:T(8,128)(2,1)}, bf16[5,32,128]{2,1,0:T(8,128)(2,1)S(1)}, u32[]{:S(2)}, u32[]{:S(2)}) %collective-permute-start) | collective-permute-done | bytes 40992 | tf_op jit(solution)/shard_map/ppermute | solution.py:523
  10.1 0.3 right_side.1
  10.3 22.5 %all-gather.1.sent_ref = f32[16,125,128]{2,1,0:T(8,128)S(1)} all-gather(f32[1,125,128]{2,1,0:T(8,128)S(1)} %bitcast.1), channel_id=2, replica_groups=mesh['line'=16,'cross'=32] {'line'}, dimensions={0}, use_global_device_ids=true | all-gather | bytes 1088000 | tf_op jit(solution)/shard_map/all_gather | solution.py:552
  32.8 1.8 %solve.1 = f32[5,32,128]{2,1,0:T(8,128)S(1)} custom-call(f32[16,125,128]{2,1,0:T(8,128)S(1)} %all-gather.1.sent_ref, f32[5,5,32,128]{3,2,1,0:T(8,128)S(1)} %get-tuple-element.13.jac_ref, f32[32,128]{1,0:T(8,128)S(1)} %get-tuple-element.14.step_ref, f32[4600,128]{1,0:T(8,128)S(1)} %get-tuple-element.17.fac_ref, f32[240,128]{1,0:T(8,128)S(1)} %get-tuple-element.20.val_ref), custom_call_target="tpu_custom_call" | custom-call | tf_op jit(solution)/shard_map/solve/pallas_call | solution.py:503
  34.7 0.6 %copy.5 = f32[5,32,128]{2,1,0:T(8,128)} copy(f32[5,32,128]{2,1,0:T(8,128)S(1)} %solve.1) | data formatting | bytes 163840
Async XLA Ops:
  0.0 9.6 %collective-permute-start.1 = (bf16[5,32,128]{2,1,0:T(8,128)(2,1)}, bf16[5,32,128]{2,1,0:T(8,128)(2,1)S(1)}, u32[]{:S(2)}, u32[]{:S(2)}) collective-permute-start(bf16[5,32,128]{2,1,0:T(8,128)(2,1)} %flux_hbm.1), channel_id=1, source_target_pairs={{1,2},{2,1},{3,4},{4,3},{5,6},{6,5},{7,8},{8,7},{9,10},{10,9},{11,... | collective-permute-start | bytes 122888 | tf_op jit(solution)/shard_map/ppermute | solution.py:523
  5.1 5.0 %collective-permute-start = (bf16[5,32,128]{2,1,0:T(8,128)(2,1)}, bf16[5,32,128]{2,1,0:T(8,128)(2,1)S(1)}, u32[]{:S(2)}, u32[]{:S(2)}) collective-permute-start(bf16[5,32,128]{2,1,0:T(8,128)(2,1)} %flux_hbm.1), channel_id=1, source_target_pairs={{0,1},{1,0},{2,3},{3,2},{4,5},{5,4},{6,7},{7,6},{8,9},{9,8},{10,11... | collective-permute-start | bytes 122888 | tf_op jit(solution)/shard_map/ppermute | solution.py:523

commit v6 on v4

--- a/solution.py
+++ b/solution.py
@@ -157,10 +157,10 @@
     if 2 * distance != CHUNKS:
         vlow_after, vupp_after = mturn(vlow, -distance), mturn(vupp, -distance)
     return (
-        negative(mm(low, vlow_before)),
+        mm(low, vlow_before),
         minus(own, mm(low, vupp_before)),
         minus(nxt, mm(upp, vlow_after)),
-        negative(mm(upp, vupp_after)),
+        mm(upp, vupp_after),
     )
 
 
@@ -171,7 +171,8 @@
     keep(fac_ref, base + UPP, upp)
     keep(fac_ref, base + VLOW, vlow)
     keep(fac_ref, base + VUPP, vupp)
-    return next_rows(low, own, nxt, upp, vlow, vupp, distance)
+    low, own, nxt, upp = next_rows(low, own, nxt, upp, vlow, vupp, distance)
+    return negative(low), own, nxt, negative(upp)
 
 
 def stage_rhs(fac_ref, base, own, nxt, distance):
@@ -413,11 +414,11 @@
     keep_vector(x_ref, 4, value)
     cross = mm(packed_block(1, 0), m_even)
     own = minus(packed_block(1, 25), mm(cross, vupp))
-    low = negative(mm(cross, vlow))
+    low = mm(cross, vlow)
     own_rhs = vminus(packed_vector(1, 115), mv(cross, value))
     back = packed_block(0, 75)
     nxt = minus(packed_block(0, 50), mm(back, vlow))
-    upp = negative(mm(back, vupp))
+    upp = mm(back, vupp)
     nxt_rhs = vminus(packed_vector(0, 120), mv(back, value))
     first, last = row == 0, row == CHUNKS - 1
     low = mm(low, mturn(m_odd, 1))
@@ -428,8 +429,8 @@
     nxt_rhs = [jnp.where(last, 0.0, turn(nxt_rhs[a], -1)) for a in N]
     for distance in (1, 2, 4):
         value, (vlow, vupp) = solved(plus(own, nxt), vplus(own_rhs, nxt_rhs), low, upp)
-        own_rhs = vminus(own_rhs, mv(low, vturn(value, distance)))
-        nxt_rhs = vminus(nxt_rhs, mv(upp, vturn(value, -distance)))
+        own_rhs = vplus(own_rhs, mv(low, vturn(value, distance)))
+        nxt_rhs = vplus(nxt_rhs, mv(upp, vturn(value, -distance)))
         low, own, nxt, upp = next_rows(low, own, nxt, upp, vlow, vupp, distance)
     x = solved(plus(own, nxt), vplus(own_rhs, nxt_rhs))[0]
     w_odd = mv(m_odd, x)

time: 35.5 us -> 35.5 us (level)
  no operation moved by 1% of the time
where the time goes in v6:
time: 35.5 us; the launch traced here: 35.3 us
  blocking collectives  22.5 us (63%)
  starting transfers between devices  7.03 us (20%)
  Pallas kernels  4.9 us (14%)
  local copies, waits for them, and re-layouts  0.64 us (2%)
    all_gather x1, blocking collectives, shards(): packets = lax.all_gather(packet, 'line', axis=0)  22.5 us
    ppermute x2, starting transfers between devices, shards(): lax.ppermute(cross_flux, 'cross', [pair for i in range(start, count - 1,...  7.03 us
    pallas_call x3, Pallas kernels, run(): pl.pallas_call(kernel, out_shape=outs, in_specs=[HBM] * far_args + [VMEM]...  4.9 us
  transfers between devices with their start and end apart: 2, of which 1 were waited for; matrix products, arithmetic and copies ran while one was open for 0% of the time, Pallas kernels for 8%

profile of v6, /device:TPU:199, one launch (start us, length us, event | category | flops | bytes accessed | tf_op | source)
XLA Modules:
  0.0 35.3 jit_solution(14237941867526031153)
XLA Ops:
  0.0 5.1 %collective-permute-start.1 = (bf16[5,32,128]{2,1,0:T(8,128)(2,1)}, bf16[5,32,128]{2,1,0:T(8,128)(2,1)S(1)}, u32[]{:S(2)}, u32[]{:S(2)}) collective-permute-start(bf16[5,32,128]{2,1,0:T(8,128)(2,1)} %flux_hbm.1), channel_id=1, source_target_pairs={{1,2},{2,1},{3,4},{4,3},{5,6},{6,5},{7,8},{8,7},{9,10},{10,9},{11,... | collective-permute-start | bytes 122888 | tf_op jit(solution)/shard_map/ppermute | solution.py:524
  5.1 1.9 %collective-permute-start = (bf16[5,32,128]{2,1,0:T(8,128)(2,1)}, bf16[5,32,128]{2,1,0:T(8,128)(2,1)S(1)}, u32[]{:S(2)}, u32[]{:S(2)}) collective-permute-start(bf16[5,32,128]{2,1,0:T(8,128)(2,1)} %flux_hbm.1), channel_id=1, source_target_pairs={{0,1},{1,0},{2,3},{3,2},{4,5},{5,4},{6,7},{7,6},{8,9},{9,8},{10,11... | collective-permute-start | bytes 122888 | tf_op jit(solution)/shard_map/ppermute | solution.py:524
  7.0 2.8 %factor.1 = (f32[5,5,32,128]{3,2,1,0:T(8,128)S(1)}, f32[32,128]{1,0:T(8,128)S(1)}, bf16[5,32,128]{2,1,0:T(8,128)(2,1)S(1)}, bf16[5,32,128]{2,1,0:T(8,128)(2,1)S(...) custom-call(f32[5,5,32,128]{3,2,1,0:T(8,128)} %jac_hbm.1, f32[32,128]{1,0:T(8,128)} %step_hbm.1, ...), custom_call_target="tpu_custom_call" | custom-call | tf_op jit(solution)/shard_map/factor/pallas_call | solution.py:504
  9.9 0.0 collective-permute-done.1.odd_ref
  9.9 0.2 collective-permute-done.even_ref
  10.1 0.3 right_side.1
  10.4 22.5 %all-gather.1.sent_ref = f32[16,125,128]{2,1,0:T(8,128)S(1)} all-gather(f32[1,125,128]{2,1,0:T(8,128)S(1)} %bitcast.1), channel_id=2, replica_groups=mesh['line'=16,'cross'=32] {'line'}, dimensions={0}, use_global_device_ids=true | all-gather | bytes 1088000 | tf_op jit(solution)/shard_map/all_gather | solution.py:553
  32.9 1.8 %solve.1 = f32[5,32,128]{2,1,0:T(8,128)S(1)} custom-call(f32[16,125,128]{2,1,0:T(8,128)S(1)} %all-gather.1.sent_ref, f32[5,5,32,128]{3,2,1,0:T(8,128)S(1)} %get-tuple-element.13.jac_ref, f32[32,128]{1,0:T(8,128)S(1)} %get-tuple-element.14.step_ref, f32[5600,128]{1,0:T(8,128)S(1)} %get-tuple-element.17.fac_ref, f32[280,128]{1,0:T(8,128)S(1)} %get-tuple-element.20.val_ref), custom_call_target="tpu_custom_call" | custom-call | tf_op jit(solution)/shard_map/solve/pallas_call | solution.py:504
  34.7 0.6 %copy.5 = f32[5,32,128]{2,1,0:T(8,128)} copy(f32[5,32,128]{2,1,0:T(8,128)S(1)} %solve.1) | data formatting | bytes 163840
Async XLA Ops:
  0.0 9.9 %collective-permute-start.1 = (bf16[5,32,128]{2,1,0:T(8,128)(2,1)}, bf16[5,32,128]{2,1,0:T(8,128)(2,1)S(1)}, u32[]{:S(2)}, u32[]{:S(2)}) collective-permute-start(bf16[5,32,128]{2,1,0:T(8,128)(2,1)} %flux_hbm.1), channel_id=1, source_target_pairs={{1,2},{2,1},{3,4},{4,3},{5,6},{6,5},{7,8},{8,7},{9,10},{10,9},{11,... | collective-permute-start | bytes 122888 | tf_op jit(solution)/shard_map/ppermute | solution.py:524
  5.1 5.0 %collective-permute-start = (bf16[5,32,128]{2,1,0:T(8,128)(2,1)}, bf16[5,32,128]{2,1,0:T(8,128)(2,1)S(1)}, u32[]{:S(2)}, u32[]{:S(2)}) collective-permute-start(bf16[5,32,128]{2,1,0:T(8,128)(2,1)} %flux_hbm.1), channel_id=1, source_target_pairs={{0,1},{1,0},{2,3},{3,2},{4,5},{5,4},{6,7},{7,6},{8,9},{9,8},{10,11... | collective-permute-start | bytes 122888 | tf_op jit(solution)/shard_map/ppermute | solution.py:524
